TPU v7x, 32 devices: a whole 2x2x4 slice. The times are simulated.
32 devices in a mesh: dp: 1, ctx: 32 (over z, y, x, core).
Axes of the slice: x: 2, y: 2, z: 4, core: 2. Of those that a mesh axis runs over, the one named last changes fastest.
Arguments:
- queries: bfloat16 [4096, 8192], P(('dp', 'ctx')), may hold values from -16 to 16
- out_grad: bfloat16 [4096, 8192], P(('dp', 'ctx')), may hold values from -6 to 6
- enc_states: bfloat16 [384, 1024], P(('dp', 'ctx')), may hold values from -8 to 8
- w_key: bfloat16 [1024, 8192], P('dp', 'ctx'), may hold values from -1 to 1
- w_value: bfloat16 [1024, 8192], P('dp', 'ctx'), may hold values from -0.1875 to 0.1875
- dec_segments: int32 [4096], P(('dp', 'ctx')), may hold values from 0 to 3, as said below
- enc_segments: int32 [384], P(('dp', 'ctx')), may hold values from 0 to 3, as said below
Outputs:
- query_grad: bfloat16 [4096, 8192], P(('dp', 'ctx'))
- enc_grad: bfloat16 [384, 1024], P(('dp', 'ctx'))
- w_key_grad: float32 [1024, 8192], P('dp', 'ctx')
- w_value_grad: float32 [1024, 8192], P('dp', 'ctx')
Inputs may be any that keep to these rules, and one draw needn't show every extreme that they name: `dec_segments`: within each pack the ids never fall along the tokens, and each of the 4 ids has one or more decoder tokens in the pack. `enc_segments`: within each pack the ids never fall along the tokens, and each of the 4 ids has two or more encoder tokens in the pack.
All inputs are finite; a program needn't handle non-finite values.
Results may differ from a plain program's by a relative error of at most 0.019.
Values may be sent and summed in bfloat16 or wider, within the bound.
A program may use at most 64 MiB of HBM per device.

v0:
```python
import math

import jax
import jax.numpy as jnp
from jax import lax
from jax.sharding import PartitionSpec as P

HEAD_DIM = 128


def attend(queries, out_grads, key_rows, value_rows, query_ids, key_ids):
    length, full_width = queries.shape
    key_count = key_rows.shape[0]
    head_count = full_width // HEAD_DIM
    group_size = min(head_count, 16)
    column_count = group_size * HEAD_DIM
    row_count = math.gcd(length, 1024)

    def head_group(number):
        column_start = number * column_count
        key_block = key_rows.reshape(key_count, group_size, HEAD_DIM)
        value_block = value_rows.reshape(key_count, group_size, HEAD_DIM)

        def query_block(totals, block_number):
            first_row = block_number * row_count
            query_part = lax.dynamic_slice(
                queries, (first_row, column_start), (row_count, column_count)
            ).reshape(row_count, group_size, HEAD_DIM)
            grad_part = lax.dynamic_slice(
                out_grads, (first_row, column_start), (row_count, column_count)
            ).reshape(row_count, group_size, HEAD_DIM)
            block_ids = lax.dynamic_slice_in_dim(query_ids, first_row, row_count, 0)
            allowed = block_ids[:, None] == key_ids[None, :]
            scores = jnp.einsum(
                "qhd,khd->hqk", query_part, key_block, preferred_element_type=jnp.float32
            )
            scores = jnp.where(allowed[None], scores, -jnp.inf)
            highest = jnp.max(scores, axis=2, keepdims=True)
            weights = jnp.exp(scores - highest)
            probability = weights / jnp.sum(weights, axis=2, keepdims=True)
            upstream = jnp.einsum(
                "qhd,khd->hqk", grad_part, value_block, preferred_element_type=jnp.float32
            )
            row_dot = jnp.sum(probability * upstream, axis=2, keepdims=True)
            score_grad = (probability * (upstream - row_dot)).astype(jnp.bfloat16)
            rounded = probability.astype(jnp.bfloat16)
            key_total = totals[0] + jnp.einsum(
                "hqk,qhd->khd", score_grad, query_part, preferred_element_type=jnp.float32
            )
            value_total = totals[1] + jnp.einsum(
                "hqk,qhd->khd", rounded, grad_part, preferred_element_type=jnp.float32
            )
            totals = (key_total, value_total)
            query_grad = jnp.einsum(
                "hqk,khd->qhd", score_grad, key_block, preferred_element_type=jnp.float32
            ).astype(jnp.bfloat16)
            return (totals, query_grad.reshape(row_count, column_count))

        zeros = jnp.zeros((key_count, group_size, HEAD_DIM), jnp.float32)
        totals, query_grads = lax.scan(
            query_block, (zeros, zeros), jnp.arange(length // row_count, dtype=jnp.int32)
        )
        results = ()
        results = results + (query_grads.reshape(length, column_count),)
        results = results + (
            totals[0].reshape(key_count, column_count),
            totals[1].reshape(key_count, column_count),
        )
        return results

    pieces = lax.map(head_group, jnp.arange(head_count // group_size, dtype=jnp.int32))
    return tuple(
        (jnp.moveaxis(piece, 0, 1).reshape(piece.shape[1], full_width) for piece in pieces)
    )


def body(queries, out_grad, enc_states, w_key, w_value, dec_segments, enc_segments):
    encoder, key_ids = (
        lax.all_gather(enc_states, "ctx", axis=0, tiled=True),
        lax.all_gather(enc_segments, "ctx", axis=0, tiled=True),
    )
    key_weight, value_weight = (
        lax.all_gather(w_key, "dp", axis=0, tiled=True),
        lax.all_gather(w_value, "dp", axis=0, tiled=True),
    )
    key_part = jnp.dot(encoder, key_weight, preferred_element_type=jnp.float32).astype(jnp.bfloat16)
    value_part = jnp.dot(encoder, value_weight, preferred_element_type=jnp.float32).astype(
        jnp.bfloat16
    )
    local_queries, local_grads = (
        lax.all_to_all(queries, "ctx", split_axis=1, concat_axis=0, tiled=True),
        lax.all_to_all(out_grad, "ctx", split_axis=1, concat_axis=0, tiled=True),
    )
    query_ids = lax.all_gather(dec_segments, "ctx", axis=0, tiled=True)
    head_grad, key_grad, value_grad = attend(
        local_queries, local_grads, key_part, value_part, query_ids, key_ids
    )
    query_grad = lax.all_to_all(head_grad, "ctx", split_axis=0, concat_axis=1, tiled=True)
    key_round = key_grad.astype(jnp.bfloat16)
    value_round = value_grad.astype(jnp.bfloat16)
    across = (((1,), (1,)), ((), ()))
    partial_value = lax.dot_general(
        key_round, key_weight, across, preferred_element_type=jnp.float32
    )
    partial_value = partial_value + lax.dot_general(
        value_round, value_weight, across, preferred_element_type=jnp.float32
    )
    enc_grad = lax.psum_scatter(
        partial_value.astype(jnp.bfloat16), "ctx", scatter_dimension=0, tiled=True
    )
    down = (((0,), (0,)), ((), ()))
    key_term = lax.dot_general(encoder, key_round, down, preferred_element_type=jnp.float32)
    value_term = lax.dot_general(encoder, value_round, down, preferred_element_type=jnp.float32)
    w_key_grad, w_value_grad = (
        lax.psum_scatter(
            key_term.astype(jnp.bfloat16), "dp", scatter_dimension=0, tiled=True
        ).astype(jnp.float32),
        lax.psum_scatter(
            value_term.astype(jnp.bfloat16), "dp", scatter_dimension=0, tiled=True
        ).astype(jnp.float32),
    )
    return (query_grad, enc_grad, w_key_grad, w_value_grad)


def solution(mesh):
    in_specs = (
        P(("dp", "ctx"), None),
        P(("dp", "ctx"), None),
        P(("dp", "ctx"), None),
        P("dp", "ctx"),
        P("dp", "ctx"),
        P(("dp", "ctx")),
        P(("dp", "ctx")),
    )
    out_specs = (P(("dp", "ctx"), None), P(("dp", "ctx"), None), P("dp", "ctx"), P("dp", "ctx"))
    return jax.shard_map(body, mesh=mesh, in_specs=in_specs, out_specs=out_specs, check_vma=False)
```

profile of v0, /device:TPU:0, one launch (start us, length us, event | category | flops | bytes accessed | tf_op | source)
XLA Modules:
  0.0 430.7 jit_solution(11465788982890251709)
XLA Ops:
  0.6 4.1 copy.68
  4.8 7.5 %all-to-all-start = ((bf16[128,32,256]{0,2,1:T(8,128)(2,1)}), bf16[128,32,256]{0,2,1:T(8,128)(2,1)}, u32[]{:S(2)}, u32[]{:S(2)}) async-start(bf16[128,32,256]{0,2,1:T(8,128)(2,1)} %bitcast.97), calls=%async_computation | async-start | bytes 4194304 | tf_op jit(solution)/shard_map/all_to_all | solution.py:91
  12.2 4.1 copy.70
  16.4 44.6 %all-to-all-done = bf16[128,32,256]{0,2,1:T(8,128)(2,1)} async-done(((bf16[128,32,256]{0,2,1:T(8,128)(2,1)}), bf16[128,32,256]{0,2,1:T(8,128)(2,1)}, u32[]{:S(2)}, u32[]{:S(2)}) %all-to-all-start) | async-done | bytes 2097184 | tf_op jit(solution)/shard_map/all_to_all | solution.py:91
  60.9 4.2 all-to-all-start.1
  65.2 73.4 %all-gather.1 = bf16[32,12,1024]{2,1,0:T(8,128)(2,1)S(1)} all-gather(bf16[1,12,1024]{2,1,0:T(8,128)(2,1)S(1)} %bitcast.107), channel_id=1, replica_groups=mesh['dp'=1,'ctx'=32] {'ctx'}, dimensions={0}, use_global_device_ids=true | all-gather | bytes 811008 | tf_op jit(solution)/shard_map/all_gather | solution.py:79
  139.4 0.8 copy.74
  140.4 42.1 %all-reduce = s32[384]{0:T(512)S(1)} all-reduce(s32[384]{0:T(512)S(1)} %dynamic-update-slice), channel_id=1, replica_groups=mesh['dp'=1,'ctx'=32] {'ctx'}, use_global_device_ids=true, to_apply=%add | all-reduce | flops 384 | bytes 3072
  182.5 40.8 %all-gather = s32[32,1,128]{2,1,0:T(1,128)S(1)} all-gather(s32[1,1,128]{2,1,0:T(1,128)S(1)} %bitcast.108), channel_id=1, replica_groups=mesh['dp'=1,'ctx'=32] {'ctx'}, dimensions={0}, use_global_device_ids=true | all-gather | bytes 16896 | tf_op jit(solution)/shard_map/all_gather | solution.py:94
  223.8 4.1 copy.69
  227.9 4.1 copy.71
  231.9 57.9 %while.27 = (s32[]{:T(128)}, f32[384,2,128]{0,2,1:T(8,128)S(1)}, f32[384,2,128]{0,2,1:T(8,128)}, bf16[4,1024,256]{2,1,0:T(8,128)(2,1)}, s32[4]{0:T(128)S(1)}, /*...) while((s32[]{:T(128)}, f32[384,2,128]{0,2,1:T(8,128)S(1)}, ...), condition=%wide.region_4.5_spmd.clone, body=%wide.region_0.4_spmd.clone.sunk | while | flops 1017117056 | bytes 52033364 | solution.py:60
  231.9 0.6 dynamic_slice.32
  233.2 1.0 broadcast_compare_fusion.2
  234.2 1.3 constant_dynamic-slice_fusion.4
  235.9 4.0 fusion.71
  239.9 2.7 fusion.73
  242.7 0.6 multiply_reduce_fusion.2
  243.5 0.8 multiply_convert_fusion.2
  244.3 0.6 fusion.72
  245.6 0.8 constant_dynamic-update-slice_fusion.2
  246.4 0.6 dynamic_slice.32
  247.7 1.0 broadcast_compare_fusion.2
  248.7 1.3 constant_dynamic-slice_fusion.4
  250.4 3.9 fusion.71
  254.4 2.7 fusion.73
  257.2 0.6 multiply_reduce_fusion.2
  258.0 0.8 multiply_convert_fusion.2
  258.8 0.6 fusion.72
  260.1 0.8 constant_dynamic-update-slice_fusion.2
  260.9 0.6 dynamic_slice.32
  262.1 1.0 broadcast_compare_fusion.2
  263.2 1.3 constant_dynamic-slice_fusion.4
  264.9 4.0 fusion.71
  268.9 2.7 fusion.73
  271.7 0.6 multiply_reduce_fusion.2
  272.4 0.8 multiply_convert_fusion.2
  273.2 0.6 fusion.72
  274.5 0.8 constant_dynamic-update-slice_fusion.2
  276.6 1.0 broadcast_compare_fusion.2
  277.7 1.3 constant_dynamic-slice_fusion.4
  279.4 4.0 fusion.71
  283.3 2.7 fusion.73
  286.2 0.6 multiply_reduce_fusion.2
  286.9 0.8 multiply_convert_fusion.2
  287.7 0.6 fusion.72
  289.0 0.8 constant_dynamic-update-slice_fusion.2
  289.8 3.6 all-to-all-start.2
  294.9 101.9 %fusion = bf16[16,1024]{1,0:T(8,128)(2,1)S(1)} fusion(bf16[384,1024]{1,0:T(8,128)(2,1)S(1)} %add_convert_fusion), kind=kCustom, calls=%all-reduce-scatter | all-reduce-scatter fusion | flops 524289 | bytes 819200
  396.8 1.3 collective-permute-start.6
  398.1 1.3 collective-permute-start.5
  399.4 1.3 collective-permute-start.7
  401.2 1.3 collective-permute-start.4
  402.5 4.8 %collective-permute-start.3 = (bf16[16,1024]{1,0:T(8,128)(2,1)S(1)}, bf16[16,1024]{1,0:T(8,128)(2,1)S(1)}, u32[]{:S(2)}, u32[]{:S(2)}) collective-permute-start(bf16[16,1024]{1,0:T(8,128)(2,1)S(1)} %fusion), channel_id=1, source_target_pairs={{0,4},{1,5},{2,6},{3,7},{4,8},{5,9},{6,10},{7,11},{8,12},{9,13},{1... | collective-permute-start | bytes 98312
  407.2 1.3 collective-permute-start.2
  408.5 6.8 %collective-permute-start.1 = (bf16[16,1024]{1,0:T(8,128)(2,1)S(1)}, bf16[16,1024]{1,0:T(8,128)(2,1)S(1)}, u32[]{:S(2)}, u32[]{:S(2)}) collective-permute-start(bf16[16,1024]{1,0:T(8,128)(2,1)S(1)} %fusion), channel_id=1, source_target_pairs={{0,2},{1,3},{2,4},{3,5},{4,6},{5,7},{6,8},{7,9},{8,10},{9,11},{10,... | collective-permute-start | bytes 98312
  415.4 1.3 collective-permute-start
  416.7 1.4 fusion.20
  418.1 1.3 copy.79
  419.4 1.3 copy.78
  420.8 1.2 concatenate
  422.0 0.6 constant_dynamic-slice_fusion.2
  422.6 4.1 copy.76
  426.7 4.1 copy.77
  (94 shorter events, 9.2 us)
Async XLA Ops:
  0.6 222.6 %copy-start = (bf16[1024,256]{1,0:T(8,128)(2,1)S(1)}, bf16[1024,256]{1,0:T(8,128)(2,1)}, u32[]{:S(2)}) copy-start(bf16[1024,256]{1,0:T(8,128)(2,1)} %param.12) | copy-start | bytes 1572868
  4.8 56.2 %all-to-all-start = ((bf16[128,32,256]{0,2,1:T(8,128)(2,1)}), bf16[128,32,256]{0,2,1:T(8,128)(2,1)}, u32[]{:S(2)}, u32[]{:S(2)}) async-start(bf16[128,32,256]{0,2,1:T(8,128)(2,1)} %bitcast.97), calls=%async_computation | async-start | bytes 4194304 | tf_op jit(solution)/shard_map/all_to_all | solution.py:91
  60.9 4.3 copy-start.9
  60.9 166.9 %all-to-all-start.1 = ((bf16[128,32,256]{0,2,1:T(8,128)(2,1)}), bf16[128,32,256]{0,2,1:T(8,128)(2,1)}, u32[]{:S(2)}, u32[]{:S(2)}) async-start(bf16[128,32,256]{0,2,1:T(8,128)(2,1)} %bitcast.96), calls=%async_computation.1 | async-start | bytes 4194304 | tf_op jit(solution)/shard_map/all_to_all | solution.py:92
  65.2 73.7 %copy-start.3 = (bf16[1024,256]{1,0:T(8,128)(2,1)S(1)}, bf16[1024,256]{1,0:T(8,128)(2,1)}, u32[]{:S(2)}) copy-start(bf16[1024,256]{1,0:T(8,128)(2,1)} %param.13) | copy-start | bytes 1572868
  138.7 1.5 copy-start.11
  138.7 43.8 %copy-start.10 = (s32[128]{0:T(128)S(1)}, s32[128]{0:T(128)}, u32[]{:S(2)}) copy-start(s32[128]{0:T(128)} %param.14) | copy-start | bytes 1540
  235.9 4.0 copy-start.5
  239.9 2.8 copy-start.1
  239.9 2.8 copy-start.8
  242.7 0.7 copy-start.6
  250.4 4.0 copy-start.5
  254.4 2.8 copy-start.1
  254.4 2.8 copy-start.8
  257.2 0.7 copy-start.6
  264.9 4.0 copy-start.5
  268.8 2.8 copy-start.1
  268.8 2.8 copy-start.8
  271.7 0.7 copy-start.6
  279.4 4.0 copy-start.5
  283.3 2.8 copy-start.1
  283.3 2.8 copy-start.8
  286.2 0.7 copy-start.6
  289.8 3.7 copy-start.7
  289.8 132.7 %all-to-all-start.2 = ((bf16[32,128,256]{2,1,0:T(8,128)(2,1)}), bf16[32,128,256]{2,1,0:T(8,128)(2,1)}, u32[]{:S(2)}, u32[]{:S(2)}) async-start(bf16[32,128,256]{2,1,0:T(8,128)(2,1)} %bitcast.100), calls=%async_computation.2 | async-start | bytes 4194304 | tf_op jit(solution)/shard_map/all_to_all | solution.py:98
  293.5 1.0 copy-start.4
  396.8 11.7 %collective-permute-start.6 = (bf16[16,1024]{1,0:T(8,128)(2,1)S(1)}, bf16[16,1024]{1,0:T(8,128)(2,1)S(1)}, u32[]{:S(2)}, u32[]{:S(2)}) collective-permute-start(bf16[16,1024]{1,0:T(8,128)(2,1)S(1)} %fusion), channel_id=1, source_target_pairs={{0,7},{1,8},{2,9},{3,10},{4,11},{5,12},{6,13},{7,14},{8,15},{9,16}... | collective-permute-start | bytes 98312
  398.1 17.3 %collective-permute-start.5 = (bf16[16,1024]{1,0:T(8,128)(2,1)S(1)}, bf16[16,1024]{1,0:T(8,128)(2,1)S(1)}, u32[]{:S(2)}, u32[]{:S(2)}) collective-permute-start(bf16[16,1024]{1,0:T(8,128)(2,1)S(1)} %fusion), channel_id=1, source_target_pairs={{0,6},{1,7},{2,8},{3,9},{4,10},{5,11},{6,12},{7,13},{8,14},{9,15},... | collective-permute-start | bytes 98312
  399.4 7.8 %collective-permute-start.7 = (bf16[12,1024]{1,0:T(8,128)(2,1)S(1)}, bf16[12,1024]{1,0:T(8,128)(2,1)S(1)}, u32[]{:S(2)}, u32[]{:S(2)}) collective-permute-start(bf16[12,1024]{1,0:T(8,128)(2,1)S(1)} %slice), channel_id=1, source_target_pairs={{0,8},{1,9},{2,10},{3,11},{4,12},{5,13},{6,14},{7,15},{8,16},{9,17... | collective-permute-start | bytes 73736
  401.2 19.6 %collective-permute-start.4 = (bf16[16,1024]{1,0:T(8,128)(2,1)S(1)}, bf16[16,1024]{1,0:T(8,128)(2,1)S(1)}, u32[]{:S(2)}, u32[]{:S(2)}) collective-permute-start(bf16[16,1024]{1,0:T(8,128)(2,1)S(1)} %fusion), channel_id=1, source_target_pairs={{0,5},{1,6},{2,7},{3,8},{4,9},{5,10},{6,11},{7,12},{8,13},{9,14},{... | collective-permute-start | bytes 98312
  402.5 18.3 %collective-permute-start.3 = (bf16[16,1024]{1,0:T(8,128)(2,1)S(1)}, bf16[16,1024]{1,0:T(8,128)(2,1)S(1)}, u32[]{:S(2)}, u32[]{:S(2)}) collective-permute-start(bf16[16,1024]{1,0:T(8,128)(2,1)S(1)} %fusion), channel_id=1, source_target_pairs={{0,4},{1,5},{2,6},{3,7},{4,8},{5,9},{6,10},{7,11},{8,12},{9,13},{1... | collective-permute-start | bytes 98312
  407.2 13.5 %collective-permute-start.2 = (bf16[16,1024]{1,0:T(8,128)(2,1)S(1)}, bf16[16,1024]{1,0:T(8,128)(2,1)S(1)}, u32[]{:S(2)}, u32[]{:S(2)}) collective-permute-start(bf16[16,1024]{1,0:T(8,128)(2,1)S(1)} %fusion), channel_id=1, source_target_pairs={{0,3},{1,4},{2,5},{3,6},{4,7},{5,8},{6,9},{7,10},{8,11},{9,12},{10... | collective-permute-start | bytes 98312
  408.5 12.2 %collective-permute-start.1 = (bf16[16,1024]{1,0:T(8,128)(2,1)S(1)}, bf16[16,1024]{1,0:T(8,128)(2,1)S(1)}, u32[]{:S(2)}, u32[]{:S(2)}) collective-permute-start(bf16[16,1024]{1,0:T(8,128)(2,1)S(1)} %fusion), channel_id=1, source_target_pairs={{0,2},{1,3},{2,4},{3,5},{4,6},{5,7},{6,8},{7,9},{8,10},{9,11},{10,... | collective-permute-start | bytes 98312
  415.4 5.4 %collective-permute-start = (bf16[16,1024]{1,0:T(8,128)(2,1)S(1)}, bf16[16,1024]{1,0:T(8,128)(2,1)S(1)}, u32[]{:S(2)}, u32[]{:S(2)}) collective-permute-start(bf16[16,1024]{1,0:T(8,128)(2,1)S(1)} %fusion), channel_id=1, source_target_pairs={{0,1},{1,2},{2,3},{3,4},{4,5},{5,6},{6,7},{7,8},{8,9},{9,10},{10,1... | collective-permute-start | bytes 98312
  418.1 1.3 copy-start.2
where the time goes:
time: 433 us; the launch traced here: 431 us
  blocking collectives  258 us (60%)
  local copies, waits for them, and re-layouts  45 us (10%)
  waiting for transfers between devices  44.6 us (10%)
  matrix products  37 us (9%)
  starting transfers between devices  34.6 us (8%)
  other arithmetic  7.34 us (2%)
    unnamed x2, blocking collectives  144 us
    all_gather x1, blocking collectives, body(): lax.all_gather(enc_states, 'ctx', axis=0, tiled=True)  73.4 us
    all_to_all x1, waiting for transfers between devices, body(): lax.all_to_all(queries, 'ctx', split_axis=1, concat_axis=0, tiled=True)  44.6 us
    all_gather x1, blocking collectives, body(): query_ids = lax.all_gather(dec_segments, 'ctx', axis=0, tiled=True)  40.8 us
    unnamed x8, starting transfers between devices  19.4 us
    unnamed x28, local copies, waits for them, and re-layouts  18.5 us
    sub x4, matrix products, query_block(): weights = jnp.exp(scores - highest)  15.8 us
    dot_general x4, matrix products, query_block(): jnp.einsum('hqk,qhd->khd', rounded, grad_part, preferred_element_type=jnp...  10.9 us
  transfers between devices with their start and end apart: 11, of which 1 were waited for; matrix products, arithmetic and copies ran while one was open for 28% of the time, Pallas kernels for 0%

commit v1 on v0

v1 whole, which is shorter than its diff:
```python
import functools

import jax
import jax.numpy as jnp
from jax import lax
from jax.experimental import pallas as pl
from jax.experimental.pallas import tpu as pltpu
from jax.sharding import PartitionSpec as P

HEAD_DIM = 128
MESH = pl.DeviceIdType.MESH
ROWS = 16


def flipped(j, s, group):
    result, weight = 0, 1
    while weight < group:
        result = result + weight * (((j // weight) + (s // weight)) % 2)
        weight *= 2
    return result


def kernel(
    planes, group, q_hbm, g_hbm, qid_ref, encx_ref, wk_ref, wv_ref, sel_ref,
    dq_out, kr_out, enc_out, eg_out,
    encbuf, qbuf, gbuf, qids, kv, kids, dqbuf, acc, own, rs_send, rs_recv,
    eg_send, eg_recv, eg2_send, eg2_recv,
    enc1_s, enc1_r, enc2_s, enc2_r, qid_s, qid_r, q_s, q_r, g_s, g_r,
    kv_s, kv_r, dq_s, dq_r, rs_s, rs_r, eg_s, eg_r, eg2_s, eg2_r,
):
    me = lax.axis_index("ctx")
    z, j = me // group, me % group
    tokens = q_hbm.shape[0]
    width = wk_ref.shape[1]
    depth = wk_ref.shape[0]
    f32, bf16 = jnp.float32, jnp.bfloat16

    def send(src, dst, s_sem, r_sem, plane, member):
        return pltpu.make_async_remote_copy(
            src_ref=src, dst_ref=dst, send_sem=s_sem, recv_sem=r_sem,
            device_id={"ctx": plane * group + member}, device_id_type=MESH,
        )

    def arrive(ref, sem):
        pltpu.make_async_copy(ref, ref, sem).wait()

    barrier = pltpu.get_barrier_semaphore()
    for s in range(1, group):
        pl.semaphore_signal(
            barrier, inc=1, device_id={"ctx": z * group + flipped(j, s, group)}, device_id_type=MESH
        )
    for d in range(1, planes):
        pl.semaphore_signal(
            barrier, inc=1, device_id={"ctx": ((z + d) % planes) * group + j}, device_id_type=MESH
        )
    pl.semaphore_wait(barrier, group - 1 + planes - 1)

    for d in range(1, planes):
        send(encx_ref, encbuf.at[z, j], enc1_s.at[d], enc1_r.at[z], (z + d) % planes, j).start()
    encbuf[z, j] = encx_ref[...]
    qids[j] = qid_ref[...]
    for d in range(1, planes):
        other = (z + d) % planes
        arrive(encbuf.at[other, j], enc1_r.at[other])
    for s in range(1, group):
        p = flipped(j, s, group)
        send(encbuf.at[:, j], encbuf.at[:, j], enc2_s.at[s], enc2_r.at[j], z, p).start()
        send(qid_ref, qids.at[j], qid_s.at[s], qid_r.at[j], z, p).start()

    def columns(zb, p):
        return pl.ds(pl.multiple_of((zb * group + p) * width, width), width)

    def launch(d, carry):
        zb = (z + d) % planes

        def to_peer(s, c):
            p = flipped(j, s, group)
            cols = columns(zb, p)
            send(q_hbm.at[:, cols], qbuf.at[zb, j], q_s.at[zb, p], q_r.at[zb, j], z, p).start()
            send(g_hbm.at[:, cols], gbuf.at[zb, j], g_s.at[zb, p], g_r.at[zb, j], z, p).start()
            return c

        pltpu.make_async_copy(q_hbm.at[:, columns(zb, j)], qbuf.at[zb, j], q_r.at[zb, j]).start()
        pltpu.make_async_copy(g_hbm.at[:, columns(zb, j)], gbuf.at[zb, j], g_r.at[zb, j]).start()
        return lax.fori_loop(1, group, to_peer, carry)

    lax.fori_loop(0, planes, launch, 0)

    for s in range(1, group):
        p = flipped(j, s, group)
        arrive(encbuf.at[:, p], enc2_r.at[p])
        arrive(qids.at[p], qid_r.at[p])
    rows = planes * group * ROWS
    encoder = encbuf[...].reshape(rows, encbuf.shape[-1])
    enc_out[...] = encoder[:, :depth]
    selector = sel_ref[...]
    key_pad = jnp.dot(encoder[:, :depth], wk_ref[...], preferred_element_type=f32).astype(bf16)
    value_pad = jnp.dot(encoder[:, :depth], wv_ref[...], preferred_element_type=f32).astype(bf16)
    kv[z, :, :width] = jnp.dot(selector, key_pad, preferred_element_type=f32).astype(bf16)
    kv[z, :, width:] = jnp.dot(selector, value_pad, preferred_element_type=f32).astype(bf16)
    kids[...] = jnp.dot(selector, encoder[:, depth:], preferred_element_type=f32)
    for d in range(1, planes):
        send(kv.at[z], kv.at[z], kv_s.at[d], kv_r.at[z], (z + planes - d) % planes, j).start()

    heads = width // HEAD_DIM
    over_rows = (((0,), (0,)), ((), ()))
    over_cols = (((1,), (1,)), ((), ()))

    def column_step(d, carry):
        zb = (z + d) % planes

        @pl.when(d > 0)
        def _():
            arrive(kv.at[zb], kv_r.at[zb])

        acc[...] = jnp.zeros_like(acc)

        def member_step(s, c):
            p = flipped(j, s, group)
            arrive(qbuf.at[zb, p], q_r.at[zb, p])
            arrive(gbuf.at[zb, p], g_r.at[zb, p])
            allowed = kids[...] == qids[p][0:1, :]
            for h in range(heads):
                lo, hi = h * HEAD_DIM, (h + 1) * HEAD_DIM
                key = kv[zb, :, lo:hi]
                value = kv[zb, :, width + lo : width + hi]
                query = qbuf[zb, p, :, lo:hi]
                grad = gbuf[zb, p, :, lo:hi]
                scores = lax.dot_general(key, query, over_cols, preferred_element_type=f32)
                scores = jnp.where(allowed, scores, -jnp.inf)
                weights = jnp.exp(scores - jnp.max(scores, axis=0, keepdims=True))
                prob = weights * (1.0 / jnp.sum(weights, axis=0, keepdims=True))
                upstream = lax.dot_general(value, grad, over_cols, preferred_element_type=f32)
                row_dot = jnp.sum(prob * upstream, axis=0, keepdims=True)
                score_grad = (prob * (upstream - row_dot)).astype(bf16)
                acc[:, lo:hi] += jnp.dot(score_grad, query, preferred_element_type=f32)
                acc[:, width + lo : width + hi] += jnp.dot(
                    prob.astype(bf16), grad, preferred_element_type=f32
                )
                dqbuf[zb, p, :, lo:hi] = lax.dot_general(
                    score_grad, key, over_rows, preferred_element_type=f32
                ).astype(bf16)

            @pl.when(s > 0)
            def _():
                send(dqbuf.at[zb, p], dq_out.at[j, zb], dq_s.at[zb, p], dq_r.at[zb, j], z, p).start()

            @pl.when(s == 0)
            def _():
                pltpu.make_async_copy(dqbuf.at[zb, p], dq_out.at[j, zb], dq_r.at[zb, j]).start()

            return c

        lax.fori_loop(0, group, member_step, 0)

        @pl.when(d == 0)
        def _():
            own[...] = acc[...]

        @pl.when(d > 0)
        def _():
            rs_send[zb] = acc[...].astype(bf16)
            send(rs_send.at[zb], rs_recv.at[z], rs_s.at[zb], rs_r.at[z], zb, j).start()

        return carry

    lax.fori_loop(0, planes, column_step, 0)

    for d in range(1, planes):
        other = (z + d) % planes
        arrive(rs_recv.at[other], rs_r.at[other])
        own[...] += rs_recv[other].astype(f32)
    total = own[...].astype(bf16)
    spread = lax.dot_general(selector, total, over_rows, preferred_element_type=f32).astype(bf16)
    kr_out[...] = spread
    for zd in range(planes):
        part = spread[zd * group * ROWS : (zd + 1) * group * ROWS]
        eg_send[zd] = (
            lax.dot_general(part[:, :width], wk_ref[...], over_cols, preferred_element_type=f32)
            + lax.dot_general(part[:, width:], wv_ref[...], over_cols, preferred_element_type=f32)
        ).astype(bf16)

    def member_rows(p):
        return eg_send.at[:, pl.ds(pl.multiple_of(p * ROWS, ROWS), ROWS), :]

    for s in range(1, group):
        p = flipped(j, s, group)
        send(member_rows(p), eg_recv.at[j], eg_s.at[p], eg_r.at[j], z, p).start()
    term = member_rows(j)[...].astype(f32)
    for s in range(1, group):
        p = flipped(j, s, group)
        arrive(eg_recv.at[p], eg_r.at[p])
        term = term + eg_recv[p].astype(f32)
    eg2_send[...] = term.astype(bf16)
    for d in range(1, planes):
        other = (z + d) % planes
        send(eg2_send.at[other], eg2_recv.at[z], eg2_s.at[other], eg2_r.at[z], other, j).start()
    final = eg2_send[z].astype(f32)
    for d in range(1, planes):
        other = (z + d) % planes
        arrive(eg2_recv.at[other], eg2_r.at[other])
        final = final + eg2_recv[other].astype(f32)
    eg_out[...] = final.astype(bf16)

    for d in range(1, planes):
        other = (z + d) % planes
        arrive(encx_ref, enc1_s.at[d])
        arrive(kv.at[z], kv_s.at[d])
        arrive(rs_send.at[other], rs_s.at[other])
        arrive(eg2_send.at[other], eg2_s.at[other])
    for s in range(1, group):
        p = flipped(j, s, group)
        arrive(encbuf.at[:, j], enc2_s.at[s])
        arrive(qid_ref, qid_s.at[s])
        arrive(member_rows(p), eg_s.at[p])

    def drain(d, carry):
        def peer(s, c):
            p = flipped(j, s, group)
            arrive(qbuf.at[d, p], q_s.at[d, p])
            arrive(gbuf.at[d, p], g_s.at[d, p])
            arrive(dqbuf.at[d, p], dq_s.at[d, p])
            arrive(dq_out.at[p, d], dq_r.at[d, p])
            return c

        arrive(dq_out.at[j, d], dq_r.at[d, j])
        return lax.fori_loop(1, group, peer, carry)

    lax.fori_loop(0, planes, drain, 0)


def body(n, queries, out_grad, enc_states, w_key, w_value, dec_segments, enc_segments):
    key_weight = lax.all_gather(w_key, "dp", axis=0, tiled=True)
    value_weight = lax.all_gather(w_value, "dp", axis=0, tiled=True)
    bf16, f32 = jnp.bfloat16, jnp.float32
    group = 8 if n % 8 == 0 else 1
    planes = n // group
    tokens = queries.shape[0]
    own_rows, depth = enc_states.shape
    width = key_weight.shape[1]
    keys = n * own_rows
    padded = n * ROWS
    ids = jnp.broadcast_to(enc_segments.astype(bf16)[:, None], (own_rows, tokens))
    encx = jnp.pad(jnp.concatenate([enc_states, ids], axis=1), ((0, ROWS - own_rows), (0, 0)))
    qid = jnp.broadcast_to(dec_segments.astype(f32)[None, :], (8, tokens))
    row = jnp.arange(keys, dtype=jnp.int32)
    place = row // own_rows * ROWS + row % own_rows
    selector = (place[:, None] == jnp.arange(padded, dtype=jnp.int32)[None, :]).astype(bf16)
    vm = pl.BlockSpec(memory_space=pltpu.VMEM)
    hbm = pl.BlockSpec(memory_space=pl.ANY)
    dma = pltpu.SemaphoreType.DMA
    pairs = (planes, group)
    dq, spread, encoder, enc_grad = pl.pallas_call(
        functools.partial(kernel, planes, group),
        out_shape=(
            jax.ShapeDtypeStruct((group, planes, tokens, width), bf16),
            jax.ShapeDtypeStruct((padded, 2 * width), bf16),
            jax.ShapeDtypeStruct((padded, depth), bf16),
            jax.ShapeDtypeStruct((ROWS, depth), bf16),
        ),
        in_specs=[hbm, hbm, vm, vm, vm, vm, vm],
        out_specs=(hbm, vm, vm, vm),
        scratch_shapes=[
            pltpu.VMEM((planes, group, ROWS, depth + tokens), bf16),
            pltpu.VMEM((planes, group, tokens, width), bf16),
            pltpu.VMEM((planes, group, tokens, width), bf16),
            pltpu.VMEM((group, 8, tokens), f32),
            pltpu.VMEM((planes, keys, 2 * width), bf16),
            pltpu.VMEM((keys, tokens), f32),
            pltpu.VMEM((planes, group, tokens, width), bf16),
            pltpu.VMEM((keys, 2 * width), f32),
            pltpu.VMEM((keys, 2 * width), f32),
            pltpu.VMEM((planes, keys, 2 * width), bf16),
            pltpu.VMEM((planes, keys, 2 * width), bf16),
            pltpu.VMEM((planes, group * ROWS, depth), bf16),
            pltpu.VMEM((group, planes, ROWS, depth), bf16),
            pltpu.VMEM((planes, ROWS, depth), bf16),
            pltpu.VMEM((planes, ROWS, depth), bf16),
            dma((planes,)), dma((planes,)), dma((group,)), dma((group,)),
            dma((group,)), dma((group,)),
            dma(pairs), dma(pairs), dma(pairs), dma(pairs),
            dma((planes,)), dma((planes,)), dma(pairs), dma(pairs),
            dma((planes,)), dma((planes,)), dma((group,)), dma((group,)),
            dma((planes,)), dma((planes,)),
        ],
        compiler_params=pltpu.CompilerParams(
            collective_id=0, has_side_effects=True, vmem_limit_bytes=48 * 1024 * 1024
        ),
    )(queries, out_grad, qid, encx, key_weight, value_weight, selector)
    query_grad = jnp.transpose(dq, (2, 1, 0, 3)).reshape(tokens, n * width)
    down = (((0,), (0,)), ((), ()))
    grads = []
    for first in (0, width):
        term = lax.dot_general(
            encoder, spread[:, first : first + width], down, preferred_element_type=f32
        )
        if lax.axis_size("dp") > 1:
            term = lax.psum_scatter(
                term.astype(bf16), "dp", scatter_dimension=0, tiled=True
            ).astype(f32)
        grads.append(term)
    return query_grad, enc_grad[:own_rows], grads[0], grads[1]


def solution(mesh):
    both = ("dp", "ctx")
    in_specs = (
        P(both, None), P(both, None), P(both, None), P("dp", "ctx"), P("dp", "ctx"), P(both), P(both),
    )
    out_specs = (P(both, None), P(both, None), P("dp", "ctx"), P("dp", "ctx"))
    return jax.shard_map(
        functools.partial(body, mesh.shape["ctx"]),
        mesh=mesh, in_specs=in_specs, out_specs=out_specs, check_vma=False,
    )
```

time: 433 us -> 142 us (0.33)
  blocking collectives: 258 us -> 0 us
  Pallas kernels: 0 us -> 126 us
  waiting for transfers between devices: 44.6 us -> 0 us
  local copies, waits for them, and re-layouts: 45 us -> 10.1 us
  starting transfers between devices: 34.6 us -> 0 us
  matrix products: 37 us -> 2.89 us
  other arithmetic: 7.34 us -> 2.23 us
    unnamed x2 -> x0, blocking collectives: 144 us -> none
    pallas_call x0 -> x1, Pallas kernels: none -> 126 us  [body(): pl.pallas_call(functools.partial(kernel, planes, group), out_shape=(jax.S...]
    all_gather x2 -> x0, blocking collectives: 114 us -> none  [the longest x1 73.4 us: body(): lax.all_gather(enc_states, 'ctx', axis=0, tiled=True)]
    all_to_all x3 -> x0, waiting for transfers between devices: 44.6 us -> none  [the longest x1 44.6 us: body(): lax.all_to_all(queries, 'ctx', split_axis=1, concat_axis=0, tiled=True)]
    unnamed x8 -> x0, starting transfers between devices: 19.4 us -> none
    dot_general x22 -> x2, matrix products: 21.2 us -> 2.89 us  [body(): lax.dot_general(encoder, spread[:, first:first + width], down, preferred_...]
    sub x4 -> x0, matrix products: 15.8 us -> none  [query_block(): weights = jnp.exp(scores - highest)]
    all_to_all x3 -> x0, starting transfers between devices: 15.3 us -> none  [the longest x1 7.45 us: body(): lax.all_to_all(queries, 'ctx', split_axis=1, concat_axis=0, tiled=True)]
  transfers between devices with their start and end apart: 11 -> 0, of which waited for: 1 -> 0; matrix products, arithmetic and copies ran while one was open for 28% -> 0% of each run, Pallas kernels for 0% -> 0%
where the time goes in v1:
time: 142 us; the launch traced here: 141 us
  Pallas kernels  126 us (89%)
  local copies, waits for them, and re-layouts  10.1 us (7%)
  matrix products  2.89 us (2%)
  other arithmetic  2.23 us (2%)
    pallas_call x1, Pallas kernels, body(): pl.pallas_call(functools.partial(kernel, planes, group), out_shape=(jax.S...  126 us
    unnamed x10, local copies, waits for them, and re-layouts  7.61 us
    dot_general x2, matrix products, body(): lax.dot_general(encoder, spread[:, first:first + width], down, preferred_...  2.89 us

profile of v1, /device:TPU:0, one launch (start us, length us, event | category | flops | bytes accessed | tf_op | source)
XLA Modules:
  0.0 141.5 jit_solution(11062606562692331498)
XLA Ops:
  0.6 0.7 convert_element_type.11
  1.3 0.7 convert_element_type.12
  2.0 0.1 broadcast_in_dim.5
  2.0 0.8 fusion.7.encx_ref
  2.8 0.1 fusion.sel_ref
  2.9 0.0 copy-start.2
  3.0 1.0 copy-done.2
  4.0 0.0 copy-start.3
  4.0 1.0 copy-done.3
  5.0 125.6 %shard_map.102 = (bf16[8,4,128,256]{3,2,1,0:T(8,128)(2,1)S(1)}, bf16[512,512]{1,0:T(8,128)(2,1)S(1)}, bf16[512,1024]{1,0:T(8,128)(2,1)S(1)}, bf16[16,1024]{1,0:T(8,128)(2,1)S(1)}) custom-call(bf16[128,8192]{1,0:T(8,128)(2,1)} %q_hbm.1, bf16[128,8192]{1,0:T(8,128)(2,1)} %g_hbm.1, f32[8,128]{1,0:T(8,128)S(1)} %broadcast_in_dim.4.qid_ref, ...), custom_call_target="tpu_custom_call" | custom-call | tf_op jit(solution)/shard_map/pallas_call | solution.py:253
  130.6 0.0 copy-start
  130.6 0.8 copy-done
  131.4 2.4 %copy.11 = bf16[128,4,8,256]{0,3,2,1:T(8,128)(2,1)} copy(bf16[128,4,8,256]{3,0,1,2:T(8,128)(2,1)S(1)} %bitcast.5) | data formatting | bytes 4194304 | tf_op jit(solution)/shard_map/transpose | solution.py:290
  133.8 0.0 copy-start.1
  133.8 4.1 %copy.12 = bf16[128,8192]{1,0:T(8,128)(2,1)} copy(bf16[128,8192]{0,1:T(8,128)(2,1)} %bitcast.7) | data formatting | bytes 4194304
  138.0 0.0 copy-done.1
  138.0 1.5 %fusion.1 = f32[1024,256]{1,0:T(8,128)} fusion(bf16[512,1024]{1,0:T(8,128)(2,1)S(1)} %get-tuple-element.10, bf16[512,512]{1,0:T(8,128)(2,1)S(1)} %copy-done.1), kind=kOutput, calls=%fused_computation.2 | convolution fusion | flops 268435456 | bytes 2359296 | tf_op jit(solution)/shard_map/dot_general | solution.py:294
  139.4 1.4 %fusion.3 = f32[1024,256]{1,0:T(8,128)} fusion(bf16[512,1024]{1,0:T(8,128)(2,1)S(1)} %get-tuple-element.10, bf16[512,512]{1,0:T(8,128)(2,1)S(1)} %copy-done.1), kind=kOutput, calls=%fused_computation.4 | convolution fusion | flops 268435456 | bytes 2359296 | tf_op jit(solution)/shard_map/dot_general | solution.py:294
  140.8 0.6 copy.14
  (2 shorter events, 0.0 us)
Async XLA Ops:
  2.9 1.0 copy-start.2
  4.0 1.0 copy-start.3
  130.6 0.8 copy-start
  133.8 4.1 %copy-start.1 = (bf16[512,512]{1,0:T(8,128)(2,1)S(1)}, bf16[512,512]{1,0:T(8,128)(2,1)}, u32[]{:S(2)}) copy-start(bf16[512,512]{1,0:T(8,128)(2,1)} %copy-done) | copy-start | bytes 1572868

commit v2 on v1

--- a/solution.py
+++ b/solution.py
@@ -21,9 +21,9 @@
 
 
 def kernel(
-    planes, group, q_hbm, g_hbm, qid_ref, encx_ref, wk_ref, wv_ref, sel_ref,
+    planes, group, q_hbm, g_hbm, qid_ref, encx_ref, wk_hbm, wv_hbm, sel_hbm,
     dq_out, kr_out, enc_out, eg_out,
-    encbuf, qbuf, gbuf, qids, kv, kids, dqbuf, acc, own, rs_send, rs_recv,
+    wk_ref, wv_ref, sel_ref, w_sem, encbuf, qbuf, gbuf, qids, kv, kids, dqbuf, acc, own, rs_send, rs_recv,
     eg_send, eg_recv, eg2_send, eg2_recv,
     enc1_s, enc1_r, enc2_s, enc2_r, qid_s, qid_r, q_s, q_r, g_s, g_r,
     kv_s, kv_r, dq_s, dq_r, rs_s, rs_r, eg_s, eg_r, eg2_s, eg2_r,
@@ -44,6 +44,12 @@
     def arrive(ref, sem):
         pltpu.make_async_copy(ref, ref, sem).wait()
 
+    loads = [
+        pltpu.make_async_copy(src, dst, w_sem.at[i])
+        for i, (src, dst) in enumerate(((wk_hbm, wk_ref), (wv_hbm, wv_ref), (sel_hbm, sel_ref)))
+    ]
+    for load in loads:
+        load.start()
     barrier = pltpu.get_barrier_semaphore()
     for s in range(1, group):
         pl.semaphore_signal(
@@ -90,6 +96,8 @@
         p = flipped(j, s, group)
         arrive(encbuf.at[:, p], enc2_r.at[p])
         arrive(qids.at[p], qid_r.at[p])
+    for load in loads:
+        load.wait()
     rows = planes * group * ROWS
     encoder = encbuf[...].reshape(rows, encbuf.shape[-1])
     enc_out[...] = encoder[:, :depth]
@@ -143,11 +151,11 @@
 
             @pl.when(s > 0)
             def _():
-                send(dqbuf.at[zb, p], dq_out.at[j, zb], dq_s.at[zb, p], dq_r.at[zb, j], z, p).start()
+                send(dqbuf.at[zb, p], dq_out.at[:, columns(zb, j)], dq_s.at[zb, p], dq_r.at[zb, j], z, p).start()
 
             @pl.when(s == 0)
             def _():
-                pltpu.make_async_copy(dqbuf.at[zb, p], dq_out.at[j, zb], dq_r.at[zb, j]).start()
+                pltpu.make_async_copy(dqbuf.at[zb, p], dq_out.at[:, columns(zb, j)], dq_r.at[zb, j]).start()
 
             return c
 
@@ -220,10 +228,10 @@
             arrive(qbuf.at[d, p], q_s.at[d, p])
             arrive(gbuf.at[d, p], g_s.at[d, p])
             arrive(dqbuf.at[d, p], dq_s.at[d, p])
-            arrive(dq_out.at[p, d], dq_r.at[d, p])
+            arrive(dq_out.at[:, columns(d, p)], dq_r.at[d, p])
             return c
 
-        arrive(dq_out.at[j, d], dq_r.at[d, j])
+        arrive(dq_out.at[:, columns(d, j)], dq_r.at[d, j])
         return lax.fori_loop(1, group, peer, carry)
 
     lax.fori_loop(0, planes, drain, 0)
@@ -253,14 +261,18 @@
     dq, spread, encoder, enc_grad = pl.pallas_call(
         functools.partial(kernel, planes, group),
         out_shape=(
-            jax.ShapeDtypeStruct((group, planes, tokens, width), bf16),
+            jax.ShapeDtypeStruct((tokens, n * width), bf16),
             jax.ShapeDtypeStruct((padded, 2 * width), bf16),
             jax.ShapeDtypeStruct((padded, depth), bf16),
             jax.ShapeDtypeStruct((ROWS, depth), bf16),
         ),
-        in_specs=[hbm, hbm, vm, vm, vm, vm, vm],
+        in_specs=[hbm, hbm, vm, vm, hbm, hbm, hbm],
         out_specs=(hbm, vm, vm, vm),
         scratch_shapes=[
+            pltpu.VMEM((depth, width), bf16),
+            pltpu.VMEM((depth, width), bf16),
+            pltpu.VMEM((keys, padded), bf16),
+            dma((3,)),
             pltpu.VMEM((planes, group, ROWS, depth + tokens), bf16),
             pltpu.VMEM((planes, group, tokens, width), bf16),
             pltpu.VMEM((planes, group, tokens, width), bf16),
@@ -287,7 +299,6 @@
             collective_id=0, has_side_effects=True, vmem_limit_bytes=48 * 1024 * 1024
         ),
     )(queries, out_grad, qid, encx, key_weight, value_weight, selector)
-    query_grad = jnp.transpose(dq, (2, 1, 0, 3)).reshape(tokens, n * width)
     down = (((0,), (0,)), ((), ()))
     grads = []
     for first in (0, width):
@@ -299,7 +310,7 @@
                 term.astype(bf16), "dp", scatter_dimension=0, tiled=True
             ).astype(f32)
         grads.append(term)
-    return query_grad, enc_grad[:own_rows], grads[0], grads[1]
+    return dq, enc_grad[:own_rows], grads[0], grads[1]
 
 
 def solution(mesh):

time: 142 us -> 136 us (0.958)
  local copies, waits for them, and re-layouts: 10.1 us -> 4.08 us
    unnamed x10 -> x6, local copies, waits for them, and re-layouts: 7.61 us -> 4.01 us
    transpose x1 -> x0, local copies, waits for them, and re-layouts: 2.42 us -> none  [body(): query_grad = jnp.transpose(dq, (2, 1, 0, 3)).reshape(tokens, n * width)]
where the time goes in v2:
time: 136 us
  Pallas kernels  126 us (93%)
  local copies, waits for them, and re-layouts  4.08 us (3%)
  matrix products  2.89 us (2%)
  other arithmetic  2.23 us (2%)
    pallas_call x1, Pallas kernels, body(): pl.pallas_call(functools.partial(kernel, planes, group), out_shape=(jax.S...  126 us
    unnamed x6, local copies, waits for them, and re-layouts  4.01 us
    dot_general x2, matrix products, body(): lax.dot_general(encoder, spread[:, first:first + width], down, preferred_...  2.89 us

profile of v2, /device:TPU:0, one launch (start us, length us, event | category | flops | bytes accessed | tf_op | source)
XLA Modules:
  0.0 135.7 jit_solution(8612144116597626964)
XLA Ops:
  0.6 0.7 convert_element_type.11
  1.3 0.7 convert_element_type.12
  2.0 0.1 broadcast_in_dim.5
  2.0 0.8 fusion.7.encx_ref
  2.8 0.1 fusion.sel_hbm
  2.9 0.0 copy-start
  3.0 1.0 copy-done
  4.0 0.0 copy-start.1
  4.0 1.0 copy-done.1
  5.0 125.9 %shard_map.102 = (bf16[128,8192]{1,0:T(8,128)(2,1)S(1)}, bf16[512,512]{1,0:T(8,128)(2,1)S(1)}, bf16[512,1024]{1,0:T(8,128)(2,1)S(1)}, bf16[16,1024]{1,0:T(8,128)(2,1)S(1)}) custom-call(bf16[128,8192]{1,0:T(8,128)(2,1)} %q_hbm.1, bf16[128,8192]{1,0:T(8,128)(2,1)} %g_hbm.1, f32[8,128]{1,0:T(8,128)S(1)} %broadcast_in_dim.4.qid_ref, ...), custom_call_target="tpu_custom_call" | custom-call | tf_op jit(solution)/shard_map/pallas_call | solution.py:261
  130.9 1.5 %fusion.1 = f32[1024,256]{1,0:T(8,128)} fusion(bf16[512,1024]{1,0:T(8,128)(2,1)S(1)} %get-tuple-element.10, bf16[512,512]{1,0:T(8,128)(2,1)S(1)} %get-tuple-element.11), kind=kOutput, calls=%fused_computation.2 | convolution fusion | flops 268435456 | bytes 2359296 | tf_op jit(solution)/shard_map/dot_general | solution.py:305
  132.4 1.4 %fusion.3 = f32[1024,256]{1,0:T(8,128)} fusion(bf16[512,1024]{1,0:T(8,128)(2,1)S(1)} %get-tuple-element.10, bf16[512,512]{1,0:T(8,128)(2,1)S(1)} %get-tuple-element.11), kind=kOutput, calls=%fused_computation.4 | convolution fusion | flops 268435456 | bytes 2359296 | tf_op jit(solution)/shard_map/dot_general | solution.py:305
  133.8 1.3 copy.13
  135.1 0.6 copy.14
  (2 shorter events, 0.0 us)
Async XLA Ops:
  2.9 1.0 copy-start
  4.0 1.0 copy-start.1
